TPU v7x, 32 devices: a whole 2x2x4 slice. The times are simulated.
32 devices in a mesh: groups: 2 (over y), seq: 4 (over z), tp: 4 (over x, core).
Axes of the slice: x: 2, y: 2, z: 4, core: 2. Of those that a mesh axis runs over, the one named last changes fastest.
Arguments:
- activations: bfloat16 [1024, 8192], P(('groups', 'seq'), 'tp'), parts along dimension 0, may hold values from -24 to 24
- queries: bfloat16 [1024, 8192], P(('groups', 'seq'), 'tp'), parts along dimension 0, may hold values from -24 to 24
- key_weight: bfloat16 [8192, 1024], P(None, 'tp'), may hold values from -0.0625 to 0.0625
- value_weight: bfloat16 [8192, 1024], P(None, 'tp'), may hold values from -0.0625 to 0.0625
- lengths: int32 [8], P('groups'), parts along dimension 0, may hold values from 1 to 320, 512 in all
- owners: int32 [32], P('groups'), parts along dimension 0, may hold values from 0 to 3, as said below
Outputs:
- attention: bfloat16 [1024, 8192], P(('groups', 'seq'), 'tp'), parts along dimension 0
- kv_cache: bfloat16 [1024, 8, 256], P(('groups', 'seq'), 'tp'), parts along dimension 0
There are 2 independent parts, one for each index of `groups`. A program takes and returns all parts, laid end to end along the dimension named above; an argument that names none is the same for every part. Nothing has to cross between parts.
Inputs may be any that keep to these rules, and one draw needn't show every extreme that they name: `owners`: every decode device is named by exactly 4 blocks; among the 4 blocks of the rows of one index of seq, no decode device is named more than 2 times, and some is named exactly 2 times.
All inputs are finite; a program needn't handle non-finite values.
Results may differ from a plain program's by a relative error of at most 0.0045.
The roundings to bfloat16 on the way count: a program that leaves them out, or rounds other values in their place, can miss the bound.
Values may be sent and summed in bfloat16 or wider, within the bound.
No kernel may reach another device: no remote copies, remote signals or barrier semaphores. Data moves between devices by JAX's collectives and lax.ppermute only.
A program may use at most 64 MiB of HBM per device.

v0:
```python
import jax
import jax.numpy as jnp
from jax import lax
from jax.sharding import PartitionSpec as P

HD = 128


def locate(row_ids, lengths):
    prompt_ends = jnp.cumsum(lengths)
    prompt_starts = prompt_ends - lengths
    segment = jnp.sum((row_ids[:, None] >= prompt_ends[None, :]).astype(jnp.int32), axis=1)
    numbers = jnp.arange(lengths.shape[0], dtype=jnp.int32)
    prompt_first = jnp.sum(
        jnp.where(segment[:, None] == numbers[None, :], prompt_starts[None, :], 0), axis=1
    )
    return (segment, row_ids - prompt_first)


def rotate(vectors, positions):
    half_size = vectors.shape[-1] // 2
    exponent = jnp.arange(half_size, dtype=jnp.float32) * (2.0 / vectors.shape[-1])
    inverse = jnp.exp(-exponent * jnp.log(jnp.float32(500000.0)))
    angles = positions.astype(jnp.float32)[:, None] * inverse[None, :]
    cosines = jnp.cos(angles)[:, None, :]
    sine_values = jnp.sin(angles)[:, None, :]
    lower_half = vectors[..., :half_size]
    upper_half = vectors[..., half_size:]
    return jnp.concatenate(
        [
            lower_half * cosines - upper_half * sine_values,
            upper_half * cosines + lower_half * sine_values,
        ],
        axis=-1,
    )


def per_device(activations, queries, key_weight, value_weight, lengths, owners):
    local_rows = activations.shape[0]
    devices = lax.axis_size("seq")
    own_index = lax.axis_index("seq")
    kv_width = key_weight.shape[1]
    kv_heads = kv_width // HD
    query_heads = queries.shape[1] // HD
    group_size = query_heads // kv_heads
    row_ids = own_index * local_rows + jnp.arange(local_rows, dtype=jnp.int32)
    segment, positions = locate(row_ids, lengths)
    portion = lax.all_gather(activations, "tp", axis=1, tiled=True)
    key_rows = key_weight
    key_sums = jnp.dot(portion, key_rows, preferred_element_type=jnp.float32)
    value_sums = jnp.dot(portion, value_weight, preferred_element_type=jnp.float32)
    keys_local = rotate(key_sums.reshape(local_rows, kv_heads, HD), positions).astype(jnp.bfloat16)
    values_local = value_sums.astype(jnp.bfloat16).reshape(local_rows, kv_heads, HD)
    packed = jnp.concatenate([keys_local, values_local], axis=-1).reshape(
        local_rows, kv_heads * 2 * HD
    )
    rotated = rotate(queries.astype(jnp.float32).reshape(local_rows, query_heads, HD), positions)
    rotated = rotated.astype(jnp.bfloat16).reshape(local_rows, kv_heads, group_size, HD)

    def attend_block(running, portion, offset):
        running_max, running_sum, running_out = running
        amount = portion.shape[0]
        paired = portion.reshape(amount, kv_heads, 2 * HD)
        key_part = paired[:, :, :HD]
        value_part = paired[:, :, HD:]
        key_rows = offset + jnp.arange(amount, dtype=jnp.int32)
        key_segment, unused = locate(key_rows, lengths)
        allowed = (
            (key_segment[None, :] == segment[:, None])
            & (key_rows[None, :] <= row_ids[:, None])
            & (key_rows[None, :] >= 0)
        )
        allowed = allowed[:, None, None, :]
        scores = jnp.einsum(
            "qhgd,khd->qhgk", rotated, key_part, preferred_element_type=jnp.float32
        ) / jnp.sqrt(jnp.float32(HD))
        new_max = jnp.maximum(running_max, jnp.max(jnp.where(allowed, scores, -1e30), axis=-1))
        weights = jnp.where(allowed, jnp.exp(scores - new_max[..., None]), 0.0)
        factor = jnp.exp(running_max - new_max)
        running_sum = running_sum * factor + jnp.sum(weights, axis=-1)
        running_out = running_out * factor[..., None] + jnp.einsum(
            "qhgk,khd->qhgd",
            weights.astype(jnp.bfloat16),
            value_part,
            preferred_element_type=jnp.float32,
        )
        return (new_max, running_sum, running_out)

    def attend(running, portion, offset):
        amount = portion.shape[0]
        if amount > 512 and amount % 512 == 0:

            def advance(carried, entry):
                sub_portion, sub_offset = entry
                return (attend_block(carried, sub_portion, offset + sub_offset), None)

            offsets = jnp.arange(amount // 512, dtype=jnp.int32) * 512
            running, unused = lax.scan(
                advance, running, (portion.reshape(amount // 512, 512, portion.shape[1]), offsets)
            )
            return running
        return attend_block(running, portion, offset)

    initial = (
        jnp.full((local_rows, kv_heads, group_size), -1e30, jnp.float32),
        jnp.zeros((local_rows, kv_heads, group_size), jnp.float32),
        jnp.zeros((local_rows, kv_heads, group_size, HD), jnp.float32),
    )
    blocks_dev = owners.shape[0] // devices
    block_len = local_rows // blocks_dev
    is_own = owners == own_index
    ordinal = jnp.cumsum(is_own.astype(jnp.int32)) - 1
    matches = is_own[None, :] & (
        ordinal[None, :] == jnp.arange(blocks_dev, dtype=jnp.int32)[:, None]
    )
    leading = jnp.sum(
        jnp.where(matches, jnp.arange(owners.shape[0], dtype=jnp.int32)[None, :], 0), axis=1
    )
    within = jnp.arange(local_rows, dtype=jnp.int32)
    wanted = jnp.repeat(leading, block_len) * block_len + within % block_len
    portion = lax.all_gather(packed, "seq", axis=0, tiled=True)
    amount = portion.shape[0]
    choose = (wanted[:, None] == jnp.arange(amount, dtype=jnp.int32)[None, :]).astype(jnp.bfloat16)
    running = attend(
        (initial, jnp.zeros((local_rows, packed.shape[1]), jnp.float32))[0], portion, jnp.int32(0)
    )
    taken = jnp.dot(choose, portion, preferred_element_type=jnp.float32)
    kv_cache = taken.astype(jnp.bfloat16).reshape(local_rows, kv_heads, 2 * HD)
    running_max, running_sum, running_out = running
    attention = (
        (running_out / running_sum[..., None])
        .astype(jnp.bfloat16)
        .reshape(local_rows, query_heads * HD)
    )
    return (attention, kv_cache)


def solution(mesh):
    in_specs = (
        P(("groups", "seq"), "tp"),
        P(("groups", "seq"), "tp"),
        P(None, "tp"),
        P(None, "tp"),
        P("groups"),
        P("groups"),
    )
    out_specs = (P(("groups", "seq"), "tp"), P(("groups", "seq"), "tp", None))
    return jax.shard_map(
        per_device, mesh=mesh, in_specs=in_specs, out_specs=out_specs, check_vma=False
    )
```

profile of v0, /device:TPU:0, one launch (start us, length us, event | category | flops | bytes accessed | tf_op | source)
XLA Modules:
  0.0 71.7 jit_solution(17123226598475692947)
XLA Ops:
  7.2 0.0 copy-start.2
  7.2 0.0 copy-start.3
  7.2 0.0 all-gather.2.cloned.1.call-start
  7.2 0.7 all-gather.2.cloned.1.call-update
  7.9 1.1 %convert_bitcast_fusion = f32[16,8,16,128]{3,1,2,0:T(8,128)S(1)} fusion(bf16[128,2048]{1,0:T(8,128)(2,1)} %param.7), kind=kLoop, calls=%fused_computation.16 | loop fusion | flops 262144 | bytes 1572864
  9.1 0.2 copy.34
  9.3 0.0 copy-done.2
  9.3 0.1 copy.26
  9.4 0.0 copy-done.3
  9.4 0.2 reduce-window.16
  9.6 0.1 add_reduce_fusion
  9.7 0.1 select_reduce_fusion
  9.8 0.1 broadcast_in_dim.57
  9.9 0.1 mul.144
  10.0 0.1 convert_reduce_fusion
  10.1 0.1 convert_reduce_fusion.1
  10.2 0.1 select_reduce_fusion.1
  10.3 0.1 fusion.23
  10.4 0.3 multiply_cosine_fusion
  10.7 0.3 fusion.31
  11.1 0.7 subtract_convert_fusion
  11.8 23.1 %all-gather.2.cloned.1.call-done = bf16[128,8192]{1,0:T(8,128)(2,1)} async-done(((bf16[128,2048]{1,0:T(8,128)(2,1)}), bf16[128,8192]{1,0:T(8,128)(2,1)}) %all-gather.2.cloned.1.call-update) | async-done | bytes 2097168 | tf_op jit(solution)/shard_map/all_gather | solution.py:48
  34.9 0.0 copy-start
  34.9 4.3 %fusion.32 = f32[128,256]{1,0:T(8,128)} fusion(bf16[128,8192]{1,0:T(8,128)(2,1)} %all-gather.2.cloned.1.call-done, bf16[8192,256]{1,0:T(8,128)(2,1)} %param.8), kind=kOutput, calls=%fused_computation.60 | convolution fusion | flops 536870912 | bytes 6422528 | tf_op jit(solution)/shard_map/dot_general | solution.py:50
  39.2 1.0 %reshape.227 = f32[128,2,128]{2,1,0:T(2,128)S(1)} reshape(f32[128,256]{1,0:T(8,128)} %fusion.32) | data formatting | bytes 262144 | tf_op jit(solution)/shard_map/reshape | solution.py:52
  40.2 0.9 %subtract_convert_fusion.1 = (bf16[128,2,64]{2,1,0:T(2,128)(2,1)S(1)}, bf16[128,2,64]{2,1,0:T(2,128)(2,1)}) fusion(f32[128,2,128]{2,1,0:T(2,128)S(1)} %reshape.227, f32[128,64]{1,0:T(8,128)S(1)} %get-tuple-element.19, f32[128,64]{1,0:T(8,128)S(1)} %get-tuple-element.18), kind=kLoop, calls=%fused_computation.32 | loop fusion | flops 131072 | bytes 262144 | tf_op jit(solution)/shard_map/convert.6
  41.1 0.0 copy-done
  41.1 0.0 copy-start.1
  41.1 2.9 %convolution_convert_fusion.1 = bf16[128,256]{1,0:T(8,128)(2,1)S(1)} fusion(bf16[128,8192]{1,0:T(8,128)(2,1)S(1)} %copy-done, bf16[8192,256]{1,0:T(8,128)(2,1)} %param.9), kind=kOutput, calls=%fused_computation.15 | convolution fusion | flops 536903680 | bytes 6356992 | tf_op jit(solution)/shard_map/dot_general | solution.py:51
  44.0 0.0 copy-done.1
  44.0 0.3 pad_maximum_fusion
  44.3 0.1 copy.21
  44.5 15.3 %all_gather.7 = bf16[512,512]{0,1:T(8,128)(2,1)S(1)} all-gather(bf16[128,512]{0,1:T(8,128)(2,1)S(1)} %bitcast.62), channel_id=1, replica_groups=mesh['groups'=2,'seq'=4,'tp'=4] {'seq'}, dimensions={0}, use_global_device_ids=true | all-gather | bytes 655360 | tf_op jit(solution)/shard_map/all_gather | solution.py:121
  59.8 1.1 %fusion = (f32[128,2,8]{0,2,1:T(8,128)S(1)}, f32[2,512,128,8]{2,1,3,0:T(8,128)S(1)}) fusion(pred[128,512]{0,1:T(8,128)(4,1)S(1)} %fusion.23, bf16[128,2,8,64]{3,0,2,1:T(8,128)(2,1)S(1)} %bitcast.61, bf16[128,2,8,64]{3,0,2,1:T(8,128)(2,1)S(1)} %bitcast.60, bf16[512,2,256]{0,2,1:T(8,128)(2,1)S(1)} %bitcast.58), kind=kOutput, calls=%fused_computation.2 | convolution fusion | flops 272627712 | bytes 5578752 | tf_op jit(solution)/shard_map/qhgd,khd->qhgk/dot_general | solution.py:74
  60.9 0.9 %fusion.3 = f32[128,2,8]{0,2,1:T(8,128)S(1)} fusion(f32[2,512,128,8]{2,1,3,0:T(8,128)S(1)} %get-tuple-element.21, f32[128,2,8]{0,2,1:T(8,128)S(1)} %broadcast_maximum_fusion, pred[128,512]{0,1:T(8,128)(4,1)S(1)} %fusion.23), kind=kLoop, calls=%fused_computation.5 | loop fusion | flops 4192256 | bytes 4276224 | tf_op jit(solution)/shard_map/reduce_sum | solution.py:80
  61.8 1.0 %divide_convert_fusion = bf16[128,2,8,128]{0,3,2,1:T(8,128)(2,1)S(1)} fusion(f32[2,512,128,8]{2,1,3,0:T(8,128)S(1)} %get-tuple-element.21, f32[128,2,8]{0,2,1:T(8,128)S(1)} %broadcast_maximum_fusion, pred[128,512]{0,1:T(8,128)(4,1)S(1)} %fusion.23, f32[128,2,8]{0,2,1:T(8,128)S(1)} %get-tuple-element.17, f32[128,2,8]{0,2,1:T(8,128)S(1)} %get-tuple-element.16, ...), kind=kOutput, calls=%fused_computation.17 | convolution fusion | flops 273416192 | bytes 5070848 | tf_op jit(solution)/shard_map/qhgk,khd->qhgd/dot_general | solution.py:81
  62.8 1.0 %copy.27 = bf16[128,2048]{1,0:T(8,128)(2,1)} copy(bf16[128,2048]{0,1:T(8,128)(2,1)S(1)} %bitcast.63) | data formatting | bytes 1048576
  63.8 0.3 convolution_convert_fusion
  64.1 0.7 reshape.235
  (11 shorter events, 0.1 us)
Async XLA Ops:
  7.2 2.1 %copy-start.2 = (s32[16]{0:T(128)S(1)}, s32[16]{0:T(128)}, u32[]{:S(2)}) copy-start(s32[16]{0:T(128)} %param.11) | copy-start | bytes 196
  7.2 2.2 %copy-start.3 = (s32[4]{0:T(128)S(1)}, s32[4]{0:T(128)}, u32[]{:S(2)}) copy-start(s32[4]{0:T(128)} %param.10) | copy-start | bytes 52
  7.2 27.7 %all-gather.2.cloned.1.call-start = ((), (), s32[]{:S(2)}) async-start(), calls=%async_computation | async-start | bytes 2621440 | tf_op jit(solution)/shard_map/all_gather | solution.py:48
  34.9 6.2 %copy-start = (bf16[128,8192]{1,0:T(8,128)(2,1)S(1)}, bf16[128,8192]{1,0:T(8,128)(2,1)}, u32[]{:S(2)}) copy-start(bf16[128,8192]{1,0:T(8,128)(2,1)} %all-gather.2.cloned.1.call-done) | copy-start | bytes 6291460
  41.1 3.0 %copy-start.1 = (bf16[128,2,64]{2,1,0:T(2,128)(2,1)S(1)}, bf16[128,2,64]{2,1,0:T(2,128)(2,1)}, u32[]{:S(2)}) copy-start(bf16[128,2,64]{2,1,0:T(2,128)(2,1)} %get-tuple-element.15) | copy-start | bytes 98308
Sparse Core Ops, SparseCore 0:
  9.6 25.2 all-gather.1
where the time goes:
time: 71.9 us; the launch traced here: 71.7 us
  waiting for transfers between devices  23.8 us (33%)
  blocking collectives  15.3 us (21%)
  between operations  14.2 us (20%)
  matrix products  9.66 us (13%)
  other arithmetic  5.07 us (7%)
  local copies, waits for them, and re-layouts  3.61 us (5%)
    all_gather x1, waiting for transfers between devices, per_device(): portion = lax.all_gather(activations, 'tp', axis=1, tiled=True)  23.1 us
    all_gather x1, blocking collectives, per_device(): portion = lax.all_gather(packed, 'seq', axis=0, tiled=True)  15.3 us
    dot_general x1, matrix products, per_device(): key_sums = jnp.dot(portion, key_rows, preferred_element_type=jnp.float32)  4.34 us
    dot_general x1, matrix products, per_device(): jnp.dot(portion, value_weight, preferred_element_type=jnp.float32)  2.93 us
    another operation x5, other arithmetic  1.78 us
  transfers between devices with their start and end apart: 1, of which 1 were waited for; matrix products, arithmetic and copies ran while one was open for 5% of the time, Pallas kernels for 0%

commit v1 on v0

--- a/solution.py
+++ b/solution.py
@@ -45,7 +45,12 @@
     group_size = query_heads // kv_heads
     row_ids = own_index * local_rows + jnp.arange(local_rows, dtype=jnp.int32)
     segment, positions = locate(row_ids, lengths)
-    portion = lax.all_gather(activations, "tp", axis=1, tiled=True)
+    ring = [activations]
+    for hop in range(3):
+        ring.append(lax.ppermute(ring[-1], "tp", [(dev, (dev + 1) % 4) for dev in range(4)]))
+    portion = jnp.roll(
+        jnp.concatenate(ring[::-1], axis=1), (lax.axis_index("tp") + 1) * ring[0].shape[1], axis=1
+    )
     key_rows = key_weight
     key_sums = jnp.dot(portion, key_rows, preferred_element_type=jnp.float32)
     value_sums = jnp.dot(portion, value_weight, preferred_element_type=jnp.float32)

time: 71.9 us -> 55.7 us (0.77)
  between operations: 14.2 us -> 0.86 us
  waiting for transfers between devices: 23.8 us -> 20.3 us
  matrix products: 9.66 us -> 6.63 us
  other arithmetic: 5.07 us -> 6.44 us
  local copies, waits for them, and re-layouts: 3.61 us -> 4.94 us
    all_gather x1 -> x0, waiting for transfers between devices: 23.1 us -> none  [per_device(): portion = lax.all_gather(activations, 'tp', axis=1, tiled=True)]
    ppermute x0 -> x3, waiting for transfers between devices: none -> 20.3 us  [per_device(): lax.ppermute(ring[-1], 'tp', [(dev, (dev + 1) % 4) for dev in range(4)])]
    dot_general x1, matrix products: 4.34 us -> 0.71 us  [per_device(): key_sums = jnp.dot(portion, key_rows, preferred_element_type=jnp.float32)]
    unnamed x10 -> x15, local copies, waits for them, and re-layouts: 1.21 us -> 3.4 us
    reshape x1, local copies, waits for them, and re-layouts: 0.97 us -> 0.07 us  [per_device(): key_sums.reshape(local_rows, kv_heads, HD)]
    another operation x5, other arithmetic: 1.78 us -> 2.51 us
  transfers between devices with their start and end apart: 1 -> 3, of which waited for: 1 -> 3; matrix products, arithmetic and copies ran while one was open for 5% -> 10% of each run, Pallas kernels for 0% -> 0%
where the time goes in v1:
time: 55.7 us; the launch traced here: 55.5 us
  waiting for transfers between devices  20.3 us (36%)
  blocking collectives  15.7 us (28%)
  matrix products  6.63 us (12%)
  other arithmetic  6.44 us (12%)
  local copies, waits for them, and re-layouts  4.94 us (9%)
  between operations  0.86 us (2%)
  starting transfers between devices  0.59 us (1%)
    ppermute x3, waiting for transfers between devices, per_device(): lax.ppermute(ring[-1], 'tp', [(dev, (dev + 1) % 4) for dev in range(4)])  20.3 us
    all_gather x1, blocking collectives, per_device(): portion = lax.all_gather(packed, 'seq', axis=0, tiled=True)  15.7 us
    dot_general x1, matrix products, per_device(): jnp.dot(portion, value_weight, preferred_element_type=jnp.float32)  3.54 us
    unnamed x15, local copies, waits for them, and re-layouts  3.4 us
    another operation x5, other arithmetic  2.51 us
    unnamed x1, other arithmetic  1.14 us
  transfers between devices with their start and end apart: 3, of which 3 were waited for; matrix products, arithmetic and copies ran while one was open for 10% of the time, Pallas kernels for 0%

profile of v1, /device:TPU:0, one launch (start us, length us, event | category | flops | bytes accessed | tf_op | source)
XLA Modules:
  0.0 55.5 jit_solution(5962415893519568963)
XLA Ops:
  0.6 0.5 collective-permute-start
  1.2 0.8 %reduce-window.16 = s32[4,1]{0,1:T(1,128)S(1)} reduce-window(s32[4,1]{0,1:T(1,128)} %bitcast.64, s32[]{:T(128)} %constant.63.clone.1), window={size=4x1 pad=3_0x0_0}, to_apply=%region_0.0 | reduce-window | flops 12 | bytes 36 | tf_op jit(solution)/shard_map/reduce-window.6
  2.0 0.7 %bitcast_subtract_fusion.1 = s32[4]{0:T(128)S(1)} fusion(s32[4]{0:T(128)} %param.10, s32[4,1]{0,1:T(1,128)S(1)} %reduce-window.16), kind=kLoop, calls=%fused_computation.69 | loop fusion | flops 4 | bytes 48 | tf_op jit(solution)/shard_map/sub | solution.py:11
  2.7 0.1 convert_reduce_fusion
  2.7 0.1 convert_reduce_fusion.1
  2.8 1.1 %convert_bitcast_fusion = f32[16,8,16,128]{3,1,2,0:T(8,128)S(1)} fusion(bf16[128,2048]{1,0:T(8,128)(2,1)} %param.7), kind=kLoop, calls=%fused_computation.20 | loop fusion | flops 262144 | bytes 1572864
  4.0 0.2 copy.34
  4.2 0.7 %convert_bitcast_fusion.1 = (s32[16,1]{0,1:T(1,128)S(1)}, pred[16]{0:T(512)(128)(4,1)S(1)}) fusion(s32[16]{0:T(128)} %param.11, s32[]{:T(128)S(6)} %axis_index.23), kind=kLoop, calls=%fused_computation.60 | loop fusion | flops 32 | bytes 148 | tf_op jit(solution)/shard_map/convert.1
  4.8 0.1 copy.26
  5.0 0.1 add_reduce_fusion
  5.1 0.1 select_reduce_fusion
  5.2 0.1 broadcast_in_dim.57
  5.3 0.1 mul.148
  5.4 0.1 select_reduce_fusion.1
  5.5 0.3 multiply_cosine_fusion
  5.8 4.4 %collective-permute-done = bf16[128,2048]{1,0:T(8,128)(2,1)S(1)} collective-permute-done((bf16[128,2048]{1,0:T(8,128)(2,1)}, bf16[128,2048]{1,0:T(8,128)(2,1)S(1)}, u32[]{:S(2)}, u32[]{:S(2)}) %collective-permute-start) | collective-permute-done | bytes 524320 | tf_op jit(solution)/shard_map/ppermute | solution.py:50
  10.2 0.0 collective-permute-start.1
  10.2 0.1 fusion.30
  10.3 0.3 fusion.40
  10.7 0.0 copy-start.2
  10.7 8.1 %collective-permute-done.1 = bf16[128,2048]{1,0:T(8,128)(2,1)S(1)} collective-permute-done((bf16[128,2048]{1,0:T(8,128)(2,1)S(1)}, bf16[128,2048]{1,0:T(8,128)(2,1)S(1)}, u32[]{:S(2)}, u32[]{:S(2)}) %collective-permute-start.1) | collective-permute-done | bytes 524320 | tf_op jit(solution)/shard_map/ppermute | solution.py:50
  18.8 0.0 collective-permute-start.2
  18.8 0.7 %subtract_convert_fusion = (bf16[128,16,64]{2,0,1:T(8,128)(2,1)S(1)}, bf16[128,16,64]{2,0,1:T(8,128)(2,1)S(1)}) fusion(f32[128,16,64]{2,1,0:T(8,128)S(1)} %get-tuple-element.13, f32[128,16,64]{2,1,0:T(8,128)S(1)} %get-tuple-element.12, f32[128,64]{1,0:T(8,128)S(1)} %get-tuple-element.19, f32[128,64]{1,0:T(8,128)S(1)} %get-tuple-element.18), kind=kLoop, calls=%fused_computation.23 | loop fusion | flops 1048576 | bytes 1638400 | tf_op jit(solution)/shard_map/convert.5
  19.5 0.0 copy-start.1
  19.5 7.9 %collective-permute-done.2 = bf16[128,2048]{1,0:T(8,128)(2,1)S(1)} collective-permute-done((bf16[128,2048]{1,0:T(8,128)(2,1)S(1)}, bf16[128,2048]{1,0:T(8,128)(2,1)S(1)}, u32[]{:S(2)}, u32[]{:S(2)}) %collective-permute-start.2) | collective-permute-done | bytes 524320 | tf_op jit(solution)/shard_map/ppermute | solution.py:50
  27.5 0.0 copy-done.2
  27.8 0.0 copy-start
  27.8 1.9 %copy-done = bf16[128,16384]{1,0:T(8,128)(2,1)} copy-done((bf16[128,16384]{1,0:T(8,128)(2,1)}, bf16[128,16384]{1,0:T(8,128)(2,1)S(1)}, u32[]{:S(2)}) %copy-start) | copy-done | bytes 4194328
  29.7 0.0 copy-done.1
  29.7 0.7 %fusion.13 = f32[128,256]{1,0:T(8,128)S(1)} fusion(bf16[8192,256]{1,0:T(8,128)(2,1)S(1)} %copy-done.1, bf16[128,16384]{1,0:T(8,128)(2,1)S(1)} %constant_dynamic-update-slice_fusion, s32[]{:T(128)S(6)} %select_n.39), kind=kOutput, calls=%fused_computation.14 | convolution fusion | flops 536870912 | bytes 6422532 | tf_op jit(solution)/shard_map/dot_general | solution.py:55
  30.4 0.1 reshape.227
  30.5 0.3 subtract_convert_fusion.1
  30.8 3.5 %fusion.21 = bf16[128,256]{1,0:T(8,128)(2,1)S(1)} fusion(bf16[8192,256]{1,0:T(8,128)(2,1)} %param.9, bf16[128,16384]{1,0:T(8,128)(2,1)} %copy-done, s32[]{:T(128)S(6)} %select_n.39), kind=kOutput, calls=%fused_computation.19 | convolution fusion | flops 536903680 | bytes 6356996 | tf_op jit(solution)/shard_map/dot_general | solution.py:56
  34.3 0.3 pad_maximum_fusion
  34.6 0.1 copy.21
  34.8 15.7 %all_gather.3 = bf16[512,512]{0,1:T(8,128)(2,1)S(1)} all-gather(bf16[128,512]{0,1:T(8,128)(2,1)S(1)} %bitcast.60), channel_id=1, replica_groups=mesh['groups'=2,'seq'=4,'tp'=4] {'seq'}, dimensions={0}, use_global_device_ids=true | all-gather | bytes 655360 | tf_op jit(solution)/shard_map/all_gather | solution.py:126
  50.5 1.1 %fusion = (f32[128,2,8]{0,2,1:T(8,128)S(1)}, f32[2,512,128,8]{2,1,3,0:T(8,128)S(1)}) fusion(pred[128,512]{0,1:T(8,128)(4,1)S(1)} %fusion.30, bf16[128,2,8,64]{3,0,2,1:T(8,128)(2,1)S(1)} %bitcast.59, bf16[128,2,8,64]{3,0,2,1:T(8,128)(2,1)S(1)} %bitcast.58, bf16[512,2,256]{0,2,1:T(8,128)(2,1)S(1)} %bitcast.56), kind=kOutput, calls=%fused_computation.2 | convolution fusion | flops 272627712 | bytes 5578752 | tf_op jit(solution)/shard_map/qhgd,khd->qhgk/dot_general | solution.py:79
  51.6 0.9 %fusion.3 = f32[128,2,8]{0,2,1:T(8,128)S(1)} fusion(f32[2,512,128,8]{2,1,3,0:T(8,128)S(1)} %get-tuple-element.21, f32[128,2,8]{0,2,1:T(8,128)S(1)} %broadcast_maximum_fusion, pred[128,512]{0,1:T(8,128)(4,1)S(1)} %fusion.30), kind=kLoop, calls=%fused_computation.5 | loop fusion | flops 4192256 | bytes 4276224 | tf_op jit(solution)/shard_map/reduce_sum | solution.py:85
  52.5 1.0 %divide_convert_fusion = bf16[128,2,8,128]{0,3,2,1:T(8,128)(2,1)S(1)} fusion(f32[2,512,128,8]{2,1,3,0:T(8,128)S(1)} %get-tuple-element.21, f32[128,2,8]{0,2,1:T(8,128)S(1)} %broadcast_maximum_fusion, pred[128,512]{0,1:T(8,128)(4,1)S(1)} %fusion.30, f32[128,2,8]{0,2,1:T(8,128)S(1)} %get-tuple-element.17, f32[128,2,8]{0,2,1:T(8,128)S(1)} %get-tuple-element.16, ...), kind=kOutput, calls=%fused_computation.21 | convolution fusion | flops 273416192 | bytes 5070848 | tf_op jit(solution)/shard_map/qhgk,khd->qhgd/dot_general | solution.py:86
  53.5 1.0 %copy.27 = bf16[128,2048]{1,0:T(8,128)(2,1)} copy(bf16[128,2048]{0,1:T(8,128)(2,1)S(1)} %bitcast.61) | data formatting | bytes 1048576
  54.5 0.3 convolution_convert_fusion
  54.8 0.7 %reshape.235 = bf16[128,2,256]{2,1,0:T(2,128)(2,1)} reshape(bf16[128,512]{1,0:T(8,128)(2,1)S(1)} %convolution_convert_fusion) | data formatting | bytes 262144 | tf_op jit(solution)/shard_map/reshape | solution.py:133
  (17 shorter events, 0.4 us)
Async XLA Ops:
  0.6 9.5 %collective-permute-start = (bf16[128,2048]{1,0:T(8,128)(2,1)}, bf16[128,2048]{1,0:T(8,128)(2,1)S(1)}, u32[]{:S(2)}, u32[]{:S(2)}) collective-permute-start(bf16[128,2048]{1,0:T(8,128)(2,1)} %param.6), channel_id=1, source_target_pairs={{0,1},{1,2},{2,3},{3,0},{4,5},{5,6},{6,7},{7,4},{8,9},{9,10},{10,1... | collective-permute-start | bytes 1572872 | tf_op jit(solution)/shard_map/ppermute | solution.py:50
  10.2 8.6 %collective-permute-start.1 = (bf16[128,2048]{1,0:T(8,128)(2,1)S(1)}, bf16[128,2048]{1,0:T(8,128)(2,1)S(1)}, u32[]{:S(2)}, u32[]{:S(2)}) collective-permute-start(bf16[128,2048]{1,0:T(8,128)(2,1)S(1)} %collective-permute-done), channel_id=1, source_target_pairs={{0,1},{1,2},{2,3},{3,0},{4,5},{5,6},{6,7},{7,4},{8,9},{9,10},{10,1... | collective-permute-start | bytes 1572872 | tf_op jit(solution)/shard_map/ppermute | solution.py:50
  10.7 16.8 %copy-start.2 = (bf16[128,2048]{1,0:T(8,128)(2,1)S(1)}, bf16[128,2048]{1,0:T(8,128)(2,1)}, u32[]{:S(2)}) copy-start(bf16[128,2048]{1,0:T(8,128)(2,1)} %param.6) | copy-start | bytes 1572868
  18.8 8.6 %collective-permute-start.2 = (bf16[128,2048]{1,0:T(8,128)(2,1)S(1)}, bf16[128,2048]{1,0:T(8,128)(2,1)S(1)}, u32[]{:S(2)}, u32[]{:S(2)}) collective-permute-start(bf16[128,2048]{1,0:T(8,128)(2,1)S(1)} %collective-permute-done.1), channel_id=1, source_target_pairs={{0,1},{1,2},{2,3},{3,0},{4,5},{5,6},{6,7},{7,4},{8,9},{9,10},{10,1... | collective-permute-start | bytes 1572872 | tf_op jit(solution)/shard_map/ppermute | solution.py:50
  19.5 10.2 %copy-start.1 = (bf16[8192,256]{1,0:T(8,128)(2,1)S(1)}, bf16[8192,256]{1,0:T(8,128)(2,1)}, u32[]{:S(2)}) copy-start(bf16[8192,256]{1,0:T(8,128)(2,1)} %param.8) | copy-start | bytes 12582916
  27.8 1.9 %copy-start = (bf16[128,16384]{1,0:T(8,128)(2,1)}, bf16[128,16384]{1,0:T(8,128)(2,1)S(1)}, u32[]{:S(2)}) copy-start(bf16[128,16384]{1,0:T(8,128)(2,1)S(1)} %constant_dynamic-update-slice_fusion) | copy-start | bytes 12582916
